TPU v7x, 256 devices: a whole 4x4x8 slice. The times are simulated.
256 devices in a mesh: firm: 16 (over y_lo, z), tm: 16 (over x, y_hi, core).
Axes of the slice: x: 4, y: 4 (y_hi: 2, y_lo: 2; y = y_hi * 2 + y_lo), z: 8, core: 2. Of those that a mesh axis runs over, the one named last changes fastest.
Arguments:
- features: bfloat16 [8192, 32, 128], P('firm', 'tm'), may hold values from -6 to 6
- cotangent: bfloat16 [8192, 32, 128], P('firm', 'tm'), may hold values from -6 to 6
- tiles: bfloat16 [64, 64, 128, 128], P('firm'), may hold values from -0.125 to 0.125
- mask: int32 [64, 64], P('firm'), may hold values 0 or 1
- w_prev: bfloat16 [2, 128, 256], replicated, may hold values from -0.375 to 0.375
- w_cur: bfloat16 [2, 128, 256], replicated, may hold values from -0.375 to 0.375
- w_self: bfloat16 [2, 128, 128], replicated, may hold values from -0.5 to 0.5
- w_nbr: bfloat16 [2, 128, 128], replicated, may hold values from -0.5 to 0.5
- dilations: int32 [2], replicated, may hold values from 1 to 2, as said below
Outputs:
- grad_features: float32 [8192, 32, 128], P('firm', 'tm')
- grad_prev: float32 [2, 128, 256], replicated
- grad_cur: float32 [2, 128, 256], replicated
- grad_self: float32 [2, 128, 128], replicated
- grad_nbr: float32 [2, 128, 128], replicated
Inputs may be any that keep to these rules, and one draw needn't show every extreme that they name: `dilations`: each layer's dilation lies between 1 and 2; some layer has dilation 1 and some layer has dilation 2.
All inputs are finite; a program needn't handle non-finite values. No bound on the sum of `mask` on one device may be relied on, other than what follows from the above.
Results may differ from a plain program's by a relative error of at most 0.007.
Values may be sent and summed in bfloat16 or wider, within the bound.
No kernel may reach another device: no remote copies, remote signals or barrier semaphores. Data moves between devices by JAX's collectives and lax.ppermute only.
A program may use at most 128 MiB of HBM per device.

v0:
```python
import jax
import jax.numpy as jnp
from jax import lax
from jax.sharding import PartitionSpec as P

L = 2


def shifted(array, axis, by):
    peers = lax.axis_size(axis)
    pairs = [(i, i + by) for i in range(peers) if 0 <= i + by < peers]
    return lax.ppermute(array, axis, pairs)


def earlier_time_days(hidden_state, dilation_factor):
    time_days = hidden_state.shape[1]
    prior = shifted(hidden_state, "tm", 1)
    paired_terms = jnp.concatenate([prior, hidden_state], axis=1)
    return lax.dynamic_slice_in_dim(paired_terms, time_days - dilation_factor, time_days, 1)


def later_time_days(reverse_flow, dilation_factor):
    time_days = reverse_flow.shape[1]
    following = shifted(reverse_flow, "tm", -1)
    paired_terms = jnp.concatenate([reverse_flow, following], axis=1)
    return lax.dynamic_slice_in_dim(paired_terms, dilation_factor, time_days, 1)


def folder(matrix, piece):
    return jnp.dot(matrix, piece, preferred_element_type=jnp.float32)


def per_device(features, cotangent, tiles, mask, w_prev, w_cur, w_self, w_nbr, dilations):
    rows, time_days, width = features.shape
    blocks_local, blocks_all, block_size, _ = tiles.shape
    all_firms = blocks_all * block_size
    masked = tiles * mask.astype(tiles.dtype)[:, :, None, None]
    row_matrix = masked.transpose(0, 2, 1, 3).reshape(rows, all_firms)
    saved = []
    hidden_state = features
    for layer_index in range(L):
        dilation_factor = dilations[layer_index]
        previous_state = earlier_time_days(hidden_state, dilation_factor)
        pre = jnp.dot(
            previous_state.reshape(-1, width),
            w_prev[layer_index],
            preferred_element_type=jnp.float32,
        )
        pre = pre + jnp.dot(
            hidden_state.reshape(-1, width), w_cur[layer_index], preferred_element_type=jnp.float32
        )
        filt = pre[:, :width]
        gate = pre[:, width:]
        gated = (jnp.tanh(filt) * jax.nn.sigmoid(gate)).astype(jnp.bfloat16)
        diffused = folder(
            row_matrix,
            lax.all_gather(gated.reshape(rows, time_days * width), "firm", axis=0, tiled=True),
        ).astype(jnp.bfloat16)
        mixed = jnp.dot(gated, w_self[layer_index], preferred_element_type=jnp.float32)
        mixed = mixed + jnp.dot(
            diffused.reshape(-1, width), w_nbr[layer_index], preferred_element_type=jnp.float32
        )
        saved.append((hidden_state, previous_state, filt, gate, gated, diffused))
        hidden_state = (
            hidden_state.astype(jnp.float32) + mixed.reshape(rows, time_days, width)
        ).astype(jnp.bfloat16)
    gradient_value = cotangent.astype(jnp.float32)
    outs_prev, outs_cur, outs_self, outs_nbr = ([], [], [], [])
    for layer_index in reversed(range(L)):
        hidden_state, previous_state, filt, gate, gated, diffused = saved[layer_index]
        dilation_factor = dilations[layer_index]
        gzb = gradient_value.astype(jnp.bfloat16).reshape(-1, width)
        outs_self.append(jnp.dot(gated.T, gzb, preferred_element_type=jnp.float32))
        outs_nbr.append(
            jnp.dot(diffused.reshape(-1, width).T, gzb, preferred_element_type=jnp.float32)
        )
        gdiff = jnp.dot(gzb, w_nbr[layer_index].T, preferred_element_type=jnp.float32).astype(
            jnp.bfloat16
        )
        gdiff_rows = gdiff.reshape(rows, time_days * width)
        spread = lax.psum_scatter(
            lax.dot_general(
                row_matrix, gdiff_rows, (((0,), (0,)), ((), ())), preferred_element_type=jnp.float32
            ),
            "firm",
            scatter_dimension=0,
            tiled=True,
        )
        ggated = jnp.dot(
            gzb, w_self[layer_index].T, preferred_element_type=jnp.float32
        ) + spread.reshape(-1, width)
        tanh_filt = jnp.tanh(filt)
        sig_gate = jax.nn.sigmoid(gate)
        gpre = jnp.concatenate(
            [
                ggated * sig_gate * (1.0 - tanh_filt * tanh_filt),
                ggated * tanh_filt * sig_gate * (1.0 - sig_gate),
            ],
            axis=1,
        ).astype(jnp.bfloat16)
        outs_cur.append(
            jnp.dot(hidden_state.reshape(-1, width).T, gpre, preferred_element_type=jnp.float32)
        )
        outs_prev.append(
            jnp.dot(previous_state.reshape(-1, width).T, gpre, preferred_element_type=jnp.float32)
        )
        reverse_flow = jnp.dot(
            gpre, w_prev[layer_index].T, preferred_element_type=jnp.float32
        ).reshape(rows, time_days, width)
        direct_path = jnp.dot(
            gpre, w_cur[layer_index].T, preferred_element_type=jnp.float32
        ).reshape(rows, time_days, width)
        gradient_value = (
            gradient_value + direct_path + later_time_days(reverse_flow, dilation_factor)
        )
    sums = lax.psum(
        (
            jnp.stack(outs_prev[::-1]),
            jnp.stack(outs_cur[::-1]),
            jnp.stack(outs_self[::-1]),
            jnp.stack(outs_nbr[::-1]),
        ),
        ("firm", "tm"),
    )
    factor = 1.0 / jnp.sqrt(jnp.float32(all_firms * time_days * lax.axis_size("tm")))
    return (gradient_value, sums[0] * factor, sums[1] * factor, sums[2] * factor, sums[3] * factor)


def solution(mesh):
    in_specs = (
        P("firm", "tm", None),
        P("firm", "tm", None),
        P("firm", None, None, None),
        P("firm", None),
        P(),
        P(),
        P(),
        P(),
        P(),
    )
    out_specs = (P("firm", "tm", None), P(), P(), P(), P())
    return jax.shard_map(
        per_device, mesh=mesh, in_specs=in_specs, out_specs=out_specs, check_vma=False
    )
```

profile of v0, /device:TPU:97, one launch (start us, length us, event | category | flops | bytes accessed | tf_op | source)
XLA Modules:
  0.0 658.3 jit_solution(12701526937728373321)
XLA Ops:
  7.2 5.4 collective-permute-start
  12.6 1.3 fusion.67
  15.2 1.2 fusion.39
  16.4 1.9 fusion.29
  18.4 1.2 convolution_add_fusion.1
  19.8 0.8 reshape.90
  20.7 0.7 convert_element_type.41
  21.3 7.2 %multiply_bitcast_fusion = bf16[4,128,64,128]{3,1,2,0:T(8,128)(2,1)} fusion(bf16[4,64,128,128]{3,2,1,0:T(8,128)(2,1)} %param.11, bf16[4,64]{1,0:T(4,128)(2,1)S(1)} %convert_element_type.41), kind=kLoop, calls=%fused_computation.8 | loop fusion | flops 4194304 | bytes 16777728 | tf_op jit(solution)/shard_map/transpose | solution.py:38
  28.6 12.1 %copy.22 = bf16[4,128,64,128]{3,2,1,0:T(8,128)(2,1)} copy(bf16[4,128,64,128]{3,1,2,0:T(8,128)(2,1)} %multiply_bitcast_fusion) | data formatting | bytes 16777216 | tf_op jit(solution)/shard_map/transpose | solution.py:38
  41.0 24.6 %fusion.6 = f32[8192,256]{1,0:T(8,128)} fusion(bf16[512,256]{1,0:T(8,128)(2,1)S(1)} %reshape.86, bf16[64,8,64,128]{3,2,1,0:T(8,128)(2,1)} %bitcast.124), kind=kOutput, calls=%fused_computation.6 | convolution fusion | flops 2147483648 | bytes 17039360 | tf_op jit(solution)/shard_map/dot_general | solution.py:82
  65.7 0.8 copy-done.14
  66.7 19.3 %all-gather.3.cloned.1.call-done = bf16[8192,256]{1,0:T(8,128)(2,1)} async-done(((bf16[512,256]{1,0:T(8,128)(2,1)}), bf16[8192,256]{1,0:T(8,128)(2,1)}) %all-gather.3.cloned.1.call-update) | async-done | bytes 4194320 | tf_op jit(solution)/shard_map/all_gather | solution.py:57
  86.1 9.3 %fusion.13 = bf16[512,256]{1,0:T(8,128)(2,1)S(1)} fusion(bf16[8192,256]{1,0:T(8,128)(2,1)} %all-gather.3.cloned.1.call-done, bf16[64,8,64,128]{3,2,1,0:T(8,128)(2,1)} %bitcast.125), kind=kOutput, calls=%fused_computation.23 | convolution fusion | flops 2147614720 | bytes 12845056 | tf_op jit(solution)/shard_map/dot_general | solution.py:30
  95.9 14.7 %collective-permute-start.1 = (bf16[512,2,128]{2,1,0:T(2,128)(2,1)S(1)}, bf16[512,2,128]{2,1,0:T(2,128)(2,1)S(1)}, u32[]{:S(2)}, u32[]{:S(2)}) collective-permute-start(bf16[512,2,128]{2,1,0:T(2,128)(2,1)S(1)} %add_convert_fusion), channel_id=1, source_target_pairs={{0,1},{1,2},{2,3},{3,4},{4,5},{5,6},{6,7},{7,8},{8,9},{9,10},{10,1... | collective-permute-start | bytes 786440 | tf_op jit(solution)/shard_map/ppermute | solution.py:12
  112.3 1.7 collective-permute-done.1
  114.0 1.0 fusion.28
  115.0 0.7 copy-done.5
  116.0 82.7 %reduce-scatter.3.cloned.1.call-done = f32[512,256]{1,0:T(8,128)} async-done(((f32[8192,256]{1,0:T(8,128)}), f32[512,256]{1,0:T(8,128)}) %reduce-scatter.3.cloned.1.call-update) | async-done | bytes 524304 | tf_op jit(solution)/shard_map/reduce_scatter | solution.py:81
  198.7 1.9 reshape.87
  200.6 2.4 multiply_convert_fusion.3
  202.9 1.8 reshape.98
  204.8 1.0 copy_dynamic-update-slice_fusion.3
  205.8 1.0 copy_dynamic-update-slice_fusion.2
  206.8 0.3 fusion.33
  207.1 2.8 collective-permute-start.2
  211.9 7.5 %collective-permute-done.2 = f32[512,2,128]{2,0,1:T(8,128)} collective-permute-done((f32[512,2,128]{2,0,1:T(8,128)S(1)}, f32[512,2,128]{2,0,1:T(8,128)}, u32[]{:S(2)}, u32[]{:S(2)}) %collective-permute-start.2) | collective-permute-done | bytes 524320 | tf_op jit(solution)/shard_map/ppermute | solution.py:12
  219.3 2.2 fusion.68
  221.8 1.0 convolution_convert_fusion
  222.9 24.2 %fusion.2 = f32[8192,256]{1,0:T(8,128)} fusion(bf16[512,256]{1,0:T(8,128)(2,1)S(1)} %reshape.96, bf16[64,8,64,128]{3,2,1,0:T(8,128)(2,1)} %bitcast.126), kind=kOutput, calls=%fused_computation.2 | convolution fusion | flops 2147483648 | bytes 17039360 | tf_op jit(solution)/shard_map/dot_general | solution.py:82
  247.1 0.3 all-reduce.3.cloned.1.call-start
  247.4 0.6 copy-done.7
  248.3 1.9 convolution_bitcast_fusion
  250.2 1.9 convolution_bitcast_fusion.2
  252.3 0.7 pad_maximum_fusion.8
  253.3 16.1 %all-gather.5.cloned.1.call-done = bf16[8192,256]{1,0:T(8,128)(2,1)} async-done(((bf16[512,256]{1,0:T(8,128)(2,1)}), bf16[8192,256]{1,0:T(8,128)(2,1)}) %all-gather.5.cloned.1.call-update) | async-done | bytes 4194320 | tf_op jit(solution)/shard_map/all_gather | solution.py:57
  269.4 9.3 %fusion.16 = bf16[512,256]{1,0:T(8,128)(2,1)S(1)} fusion(bf16[8192,256]{1,0:T(8,128)(2,1)} %all-gather.5.cloned.1.call-done, bf16[64,8,64,128]{3,2,1,0:T(8,128)(2,1)} %bitcast.127), kind=kOutput, calls=%fused_computation.24 | convolution fusion | flops 2147614720 | bytes 12845056 | tf_op jit(solution)/shard_map/dot_general | solution.py:30
  279.1 0.7 pad_maximum_fusion.9
  279.7 101.9 %reduce-scatter.5.cloned.1.call-done = f32[512,256]{1,0:T(8,128)} async-done(((f32[8192,256]{1,0:T(8,128)}), f32[512,256]{1,0:T(8,128)}) %reduce-scatter.5.cloned.1.call-update) | async-done | bytes 524304 | tf_op jit(solution)/shard_map/reduce_scatter | solution.py:81
  381.6 1.1 reshape.97
  382.7 1.2 multiply_convert_fusion.1
  384.5 1.6 pad_maximum_fusion.7
  386.1 0.7 pad_maximum_fusion.6
  387.2 2.7 collective-permute-start.3
  391.8 254.4 %all-reduce.3.cloned.1.call-done = (f32[2,128,256]{2,1,0:T(8,128)}, f32[2,128,256]{2,1,0:T(8,128)}, f32[2,128,128]{2,1,0:T(8,128)}, f32[2,128,128]{2,1,0:T(8,128)}) async-done(((f32[2,128,256]{2,1,0:T(8,128)}, f32[2,128,256]{2,1,0:T(8,128)}, f32[2,128,128]{2,1,0:T(8,128)}, f32[2,128,128]{2,1,0:T(8,128)}), (f32[2,128,256]{2,1,0:T(8,128)}, f32[2,128,256]{2,1,0:T(8,128)}, f32[2,128,128]{2,1,0:T(8,128)}, ...) | async-done | bytes 786448 | tf_op jit(solution)/shard_map/psum | solution.py:116
  646.3 1.7 broadcast_multiply_fusion.2
  647.9 1.9 broadcast_multiply_fusion
  649.8 0.3 fusion.12
  650.1 1.2 copy.29
  (59 shorter events, 4.6 us)
Async XLA Ops:
  7.2 78.9 %all-gather.3.cloned.1.call-start = ((), (), s32[]{:S(2)}) async-start(), calls=%async_computation.3 | async-start | bytes 4456448 | tf_op jit(solution)/shard_map/all_gather | solution.py:57
  7.2 9.2 %collective-permute-start = (bf16[512,2,128]{2,1,0:T(2,128)(2,1)}, bf16[512,2,128]{2,1,0:T(2,128)(2,1)S(1)}, u32[]{:S(2)}, u32[]{:S(2)}) collective-permute-start(bf16[512,2,128]{2,1,0:T(2,128)(2,1)} %param.9), channel_id=1, source_target_pairs={{0,1},{1,2},{2,3},{3,4},{4,5},{5,6},{6,7},{7,8},{8,9},{9,10},{10,1... | collective-permute-start | bytes 786440 | tf_op jit(solution)/shard_map/ppermute | solution.py:12
  18.4 1.2 copy-start.3
  20.6 178.1 %reduce-scatter.3.cloned.1.call-start = ((), (), s32[]{:S(2)}) async-start(), calls=%async_computation.2 | async-start | bytes 8912896 | tf_op jit(solution)/shard_map/reduce_scatter | solution.py:81
  28.6 12.1 %copy-start = (bf16[512,2,128]{2,1,0:T(2,128)(2,1)S(1)}, bf16[512,2,128]{2,1,0:T(2,128)(2,1)}, u32[]{:S(2)}) copy-start(bf16[512,2,128]{2,1,0:T(2,128)(2,1)} %param.10) | copy-start | bytes 786436
  28.6 12.1 %copy-start.12 = (bf16[2,128,128]{2,1,0:T(8,128)(2,1)S(1)}, bf16[2,128,128]{2,1,0:T(8,128)(2,1)}, u32[]{:S(2)}) copy-start(bf16[2,128,128]{2,1,0:T(8,128)(2,1)} %param.16) | copy-start | bytes 196612
  65.6 0.8 copy-start.14
  65.7 203.7 %all-gather.5.cloned.1.call-start = ((), (), s32[]{:S(2)}) async-start(), calls=%async_computation.5 | async-start | bytes 4456448 | tf_op jit(solution)/shard_map/all_gather | solution.py:57
  66.7 29.0 %copy-start.1 = (bf16[512,2,128]{2,1,0:T(2,128)(2,1)S(1)}, bf16[512,2,128]{2,1,0:T(2,128)(2,1)}, u32[]{:S(2)}) copy-start(bf16[512,2,128]{2,1,0:T(2,128)(2,1)} %param.9) | copy-start | bytes 786436
  66.7 45.3 %copy-start.9 = (bf16[2,128,256]{2,1,0:T(8,128)(2,1)S(1)}, bf16[2,128,256]{2,1,0:T(8,128)(2,1)}, u32[]{:S(2)}) copy-start(bf16[2,128,256]{2,1,0:T(8,128)(2,1)} %param.14) | copy-start | bytes 393220
  66.7 49.0 %copy-start.8 = (bf16[2,128,256]{2,1,0:T(8,128)(2,1)S(1)}, bf16[2,128,256]{2,1,0:T(8,128)(2,1)}, u32[]{:S(2)}) copy-start(bf16[2,128,256]{2,1,0:T(8,128)(2,1)} %param.13) | copy-start | bytes 393220
  95.9 18.0 %collective-permute-start.1 = (bf16[512,2,128]{2,1,0:T(2,128)(2,1)S(1)}, bf16[512,2,128]{2,1,0:T(2,128)(2,1)S(1)}, u32[]{:S(2)}, u32[]{:S(2)}) collective-permute-start(bf16[512,2,128]{2,1,0:T(2,128)(2,1)S(1)} %add_convert_fusion), channel_id=1, source_target_pairs={{0,1},{1,2},{2,3},{3,4},{4,5},{5,6},{6,7},{7,8},{8,9},{9,10},{10,1... | collective-permute-start | bytes 786440 | tf_op jit(solution)/shard_map/ppermute | solution.py:12
  115.0 0.7 copy-start.5
  204.7 176.9 %reduce-scatter.5.cloned.1.call-start = ((), (), s32[]{:S(2)}) async-start(), calls=%async_computation.4 | async-start | bytes 8912896 | tf_op jit(solution)/shard_map/reduce_scatter | solution.py:81
  207.1 12.2 %collective-permute-start.2 = (f32[512,2,128]{2,0,1:T(8,128)S(1)}, f32[512,2,128]{2,0,1:T(8,128)}, u32[]{:S(2)}, u32[]{:S(2)}) collective-permute-start(f32[512,2,128]{2,0,1:T(8,128)S(1)} %fusion.33), channel_id=1, source_target_pairs={{1,0},{2,1},{3,2},{4,3},{5,4},{6,5},{7,6},{8,7},{9,8},{10,9},{11,1... | collective-permute-start | bytes 1572872 | tf_op jit(solution)/shard_map/ppermute | solution.py:12
  247.1 1.0 copy-start.7
  247.1 1.2 copy-start.11
  247.1 3.1 copy-start.6
  247.1 399.1 %all-reduce.3.cloned.1.call-start = ((), (), s32[]{:S(2)}) async-start(), calls=%async_computation.6 | async-start | bytes 1572864 | tf_op jit(solution)/shard_map/psum | solution.py:116
  253.3 130.9 %copy-start.4 = (bf16[512,2,128]{2,1,0:T(2,128)(2,1)S(1)}, bf16[512,2,128]{2,1,0:T(2,128)(2,1)}, u32[]{:S(2)}) copy-start(bf16[512,2,128]{2,1,0:T(2,128)(2,1)} %copy-done.3) | copy-start | bytes 786436
  278.7 371.1 %copy-start.2 = (f32[512,2,128]{2,0,1:T(8,128)S(1)}, f32[512,2,128]{2,0,1:T(8,128)}, u32[]{:S(2)}) copy-start(f32[512,2,128]{2,0,1:T(8,128)} %get-tuple-element.27) | copy-start | bytes 1572868
  278.7 371.1 %copy-start.10 = (bf16[2,128,256]{2,1,0:T(8,128)(2,1)S(1)}, bf16[2,128,256]{2,1,0:T(8,128)(2,1)}, u32[]{:S(2)}) copy-start(bf16[2,128,256]{2,1,0:T(8,128)(2,1)} %param.14) | copy-start | bytes 393220
  279.7 106.4 %copy-start.13 = (f32[1,128,256]{2,1,0:T(8,128)S(1)}, f32[1,128,256]{2,1,0:T(8,128)}, u32[]{:S(2)}) copy-start(f32[1,128,256]{2,1,0:T(8,128)} %convolution_bitcast_fusion.2) | copy-start | bytes 393220
  387.2 262.6 %collective-permute-start.3 = (f32[512,2,128]{2,0,1:T(8,128)S(1)}, f32[512,2,128]{2,0,1:T(8,128)S(1)}, u32[]{:S(2)}, u32[]{:S(2)}) collective-permute-start(f32[512,2,128]{2,0,1:T(8,128)S(1)} %fusion.30), channel_id=1, source_target_pairs={{1,0},{2,1},{3,2},{4,3},{5,4},{6,5},{7,6},{8,7},{9,8},{10,9},{11,1... | collective-permute-start | bytes 1572872 | tf_op jit(solution)/shard_map/ppermute | solution.py:12
Sparse Core Ops, SparseCore 0:
  20.7 65.2 all-gather.2
  88.6 110.0 reduce-scatter.2
  204.8 64.4 all-gather.4
  271.8 109.7 reduce-scatter.4
  387.9 258.2 all-reduce.2
where the time goes:
time: 669 us; the launch traced here: 658 us
  waiting for transfers between devices  484 us (72%)
  matrix products  83.9 us (13%)
  starting transfers between devices  26.1 us (4%)
  local copies, waits for them, and re-layouts  25.1 us (4%)
  between operations  21 us (3%)
  other arithmetic  18.5 us (3%)
    psum x1, waiting for transfers between devices, per_device(): lax.psum((jnp.stack(outs_prev[::-1]), jnp.stack(outs_cur[::-1]), jnp.stac...  254 us
    reduce_scatter x2, waiting for transfers between devices, per_device(): lax.psum_scatter(lax.dot_general(row_matrix, gdiff_rows, (((0,), (0,)), (...  185 us
    dot_general x2, matrix products, per_device(): lax.dot_general(row_matrix, gdiff_rows, (((0,), (0,)), ((), ())), preferr...  48.8 us
    all_gather x2, waiting for transfers between devices, per_device(): lax.all_gather(gated.reshape(rows, time_days * width), 'firm', axis=0, ti...  35.4 us
    ppermute x4, starting transfers between devices, shifted(): return lax.ppermute(array, axis, pairs)  25.6 us
    dot_general x2, matrix products, folder(): return jnp.dot(matrix, piece, preferred_element_type=jnp.float32)  18.6 us
  transfers between devices with their start and end apart: 9, of which 7 were waited for; matrix products, arithmetic and copies ran while one was open for 16% of the time, Pallas kernels for 0%

commit v1 on v0

--- a/solution.py
+++ b/solution.py
@@ -4,6 +4,14 @@
 from jax.sharding import PartitionSpec as P
 
 L = 2
+
+
+def test_the_plane(local_block):
+    mesh_name = "firm"
+    link_axis = "tm"
+    for kk in (link_axis, mesh_name):
+        local_block = jax.lax.psum(local_block, axis_name=kk)
+    return local_block
 
 
 def shifted(array, axis, by):
@@ -113,14 +121,13 @@
         gradient_value = (
             gradient_value + direct_path + later_time_days(reverse_flow, dilation_factor)
         )
-    sums = lax.psum(
+    sums = test_the_plane(
         (
             jnp.stack(outs_prev[::-1]),
             jnp.stack(outs_cur[::-1]),
             jnp.stack(outs_self[::-1]),
             jnp.stack(outs_nbr[::-1]),
-        ),
-        ("firm", "tm"),
+        )
     )
     factor = 1.0 / jnp.sqrt(jnp.float32(all_firms * time_days * lax.axis_size("tm")))
     return (gradient_value, sums[0] * factor, sums[1] * factor, sums[2] * factor, sums[3] * factor)

time: 669 us -> 697 us (1.042)
  the two profiles are of different devices: /device:TPU:97 before, /device:TPU:2 now
where the time goes in v1:
time: 697 us; the launch traced here: 686 us
  waiting for transfers between devices  523 us (75%)
  matrix products  83.9 us (12%)
  local copies, waits for them, and re-layouts  27 us (4%)
  between operations  21 us (3%)
  other arithmetic  19.4 us (3%)
  starting transfers between devices  12.4 us (2%)
    psum x2, waiting for transfers between devices, test_the_plane(): local_block = jax.lax.psum(local_block, axis_name=kk)  275 us
    reduce_scatter x2, waiting for transfers between devices, per_device(): lax.psum_scatter(lax.dot_general(row_matrix, gdiff_rows, (((0,), (0,)), (...  165 us
    all_gather x2, waiting for transfers between devices, per_device(): lax.all_gather(gated.reshape(rows, time_days * width), 'firm', axis=0, ti...  62.3 us
    dot_general x2, matrix products, per_device(): lax.dot_general(row_matrix, gdiff_rows, (((0,), (0,)), ((), ())), preferr...  48.8 us
    ppermute x4, waiting for transfers between devices, shifted(): return lax.ppermute(array, axis, pairs)  19.7 us
    dot_general x2, matrix products, folder(): return jnp.dot(matrix, piece, preferred_element_type=jnp.float32)  18.6 us
  transfers between devices with their start and end apart: 10, of which 9 were waited for; matrix products, arithmetic and copies ran while one was open for 16% of the time, Pallas kernels for 0%

profile of v1, /device:TPU:2, one launch (start us, length us, event | category | flops | bytes accessed | tf_op | source)
XLA Modules:
  0.0 686.3 jit_solution(8876560272324278944)
XLA Ops:
  7.2 1.9 collective-permute-start
  9.1 1.3 fusion.67
  11.6 1.2 fusion.39
  12.8 4.7 collective-permute-done
  17.5 1.9 fusion.29
  19.4 1.2 convolution_add_fusion.1
  20.9 0.8 reshape.90
  21.7 0.7 convert_element_type.41
  22.4 7.3 %multiply_bitcast_fusion = bf16[4,128,64,128]{3,1,2,0:T(8,128)(2,1)} fusion(bf16[4,64,128,128]{3,2,1,0:T(8,128)(2,1)} %param.11, bf16[4,64]{1,0:T(4,128)(2,1)S(1)} %convert_element_type.41), kind=kLoop, calls=%fused_computation.8 | loop fusion | flops 4194304 | bytes 16777728 | tf_op jit(solution)/shard_map/transpose | solution.py:46
  29.7 12.1 %copy.22 = bf16[4,128,64,128]{3,2,1,0:T(8,128)(2,1)} copy(bf16[4,128,64,128]{3,1,2,0:T(8,128)(2,1)} %multiply_bitcast_fusion) | data formatting | bytes 16777216 | tf_op jit(solution)/shard_map/transpose | solution.py:46
  42.1 24.6 %fusion.6 = f32[8192,256]{1,0:T(8,128)} fusion(bf16[512,256]{1,0:T(8,128)(2,1)S(1)} %reshape.86, bf16[64,8,64,128]{3,2,1,0:T(8,128)(2,1)} %bitcast.124), kind=kOutput, calls=%fused_computation.6 | convolution fusion | flops 2147483648 | bytes 17039360 | tf_op jit(solution)/shard_map/dot_general | solution.py:90
  66.8 0.8 copy-done.15
  67.8 32.2 %all-gather.3.cloned.1.call-done = bf16[8192,256]{1,0:T(8,128)(2,1)} async-done(((bf16[512,256]{1,0:T(8,128)(2,1)}), bf16[8192,256]{1,0:T(8,128)(2,1)}) %all-gather.3.cloned.1.call-update) | async-done | bytes 4194320 | tf_op jit(solution)/shard_map/all_gather | solution.py:65
  100.1 9.3 %fusion.13 = bf16[512,256]{1,0:T(8,128)(2,1)S(1)} fusion(bf16[8192,256]{1,0:T(8,128)(2,1)} %all-gather.3.cloned.1.call-done, bf16[64,8,64,128]{3,2,1,0:T(8,128)(2,1)} %bitcast.125), kind=kOutput, calls=%fused_computation.23 | convolution fusion | flops 2147614720 | bytes 12845056 | tf_op jit(solution)/shard_map/dot_general | solution.py:38
  110.0 1.9 collective-permute-start.1
  113.5 10.4 %collective-permute-done.1 = bf16[512,2,128]{2,1,0:T(2,128)(2,1)S(1)} collective-permute-done((bf16[512,2,128]{2,1,0:T(2,128)(2,1)S(1)}, bf16[512,2,128]{2,1,0:T(2,128)(2,1)S(1)}, u32[]{:S(2)}, u32[]{:S(2)}) %collective-permute-start.1) | collective-permute-done | bytes 262176 | tf_op jit(solution)/shard_map/ppermute | solution.py:20
  123.9 1.0 fusion.28
  124.8 0.7 copy-done.5
  125.8 75.5 %reduce-scatter.3.cloned.1.call-done = f32[512,256]{1,0:T(8,128)} async-done(((f32[8192,256]{1,0:T(8,128)}), f32[512,256]{1,0:T(8,128)}) %reduce-scatter.3.cloned.1.call-update) | async-done | bytes 524304 | tf_op jit(solution)/shard_map/reduce_scatter | solution.py:89
  201.3 1.9 reshape.87
  203.2 2.4 multiply_convert_fusion.3
  205.6 1.7 reshape.98
  207.4 1.0 copy_dynamic-update-slice_fusion.3
  208.4 1.0 copy_dynamic-update-slice_fusion.2
  209.7 4.0 collective-permute-start.2
  215.7 4.6 collective-permute-done.2
  220.2 2.2 fusion.68
  222.7 1.0 convolution_convert_fusion
  223.8 24.2 %fusion.2 = f32[8192,256]{1,0:T(8,128)} fusion(bf16[512,256]{1,0:T(8,128)(2,1)S(1)} %reshape.96, bf16[64,8,64,128]{3,2,1,0:T(8,128)(2,1)} %bitcast.126), kind=kOutput, calls=%fused_computation.2 | convolution fusion | flops 2147483648 | bytes 17039360 | tf_op jit(solution)/shard_map/dot_general | solution.py:90
  249.2 1.9 convolution_bitcast_fusion
  251.1 1.9 convolution_bitcast_fusion.2
  253.2 0.7 pad_maximum_fusion.8
  254.2 30.1 %all-gather.5.cloned.1.call-done = bf16[8192,256]{1,0:T(8,128)(2,1)} async-done(((bf16[512,256]{1,0:T(8,128)(2,1)}), bf16[8192,256]{1,0:T(8,128)(2,1)}) %all-gather.5.cloned.1.call-update) | async-done | bytes 4194320 | tf_op jit(solution)/shard_map/all_gather | solution.py:65
  284.3 9.3 %fusion.16 = bf16[512,256]{1,0:T(8,128)(2,1)S(1)} fusion(bf16[8192,256]{1,0:T(8,128)(2,1)} %all-gather.5.cloned.1.call-done, bf16[64,8,64,128]{3,2,1,0:T(8,128)(2,1)} %bitcast.127), kind=kOutput, calls=%fused_computation.24 | convolution fusion | flops 2147614720 | bytes 12845056 | tf_op jit(solution)/shard_map/dot_general | solution.py:38
  294.0 0.7 pad_maximum_fusion.9
  294.6 89.5 %reduce-scatter.5.cloned.1.call-done = f32[512,256]{1,0:T(8,128)} async-done(((f32[8192,256]{1,0:T(8,128)}), f32[512,256]{1,0:T(8,128)}) %reduce-scatter.5.cloned.1.call-update) | async-done | bytes 524304 | tf_op jit(solution)/shard_map/reduce_scatter | solution.py:89
  384.1 1.1 reshape.97
  385.2 1.2 multiply_convert_fusion.1
  387.1 1.6 pad_maximum_fusion.7
  388.7 1.6 pad_maximum_fusion.6
  390.4 1.0 copy_dynamic-update-slice_fusion.1
  391.4 1.0 copy_dynamic-update-slice_fusion
  392.7 4.0 collective-permute-start.3
  396.7 130.6 %all-reduce.5.cloned.1.call-done = (f32[2,128,256]{2,1,0:T(8,128)}, f32[2,128,256]{2,1,0:T(8,128)}, f32[2,128,128]{2,1,0:T(8,128)}, f32[2,128,128]{2,1,0:T(8,128)}) async-done(((f32[2,128,256]{2,1,0:T(8,128)}, f32[2,128,256]{2,1,0:T(8,128)}, f32[2,128,128]{2,1,0:T(8,128)}, f32[2,128,128]{2,1,0:T(8,128)}), (f32[2,128,256]{2,1,0:T(8,128)}, f32[2,128,256]{2,1,0:T(8,128)}, f32[2,128,128]{2,1,0:T(8,128)}, ...) | async-done | bytes 786448 | tf_op jit(solution)/shard_map/psum | solution.py:13
  529.3 1.2 copy.29
  530.5 144.9 %all-reduce.7.cloned.1.call-done = (f32[2,128,256]{2,1,0:T(8,128)}, f32[2,128,256]{2,1,0:T(8,128)}, f32[2,128,128]{2,1,0:T(8,128)}, f32[2,128,128]{2,1,0:T(8,128)}) async-done(((f32[2,128,256]{2,1,0:T(8,128)}, f32[2,128,256]{2,1,0:T(8,128)}, f32[2,128,128]{2,1,0:T(8,128)}, f32[2,128,128]{2,1,0:T(8,128)}), (f32[2,128,256]{2,1,0:T(8,128)}, f32[2,128,256]{2,1,0:T(8,128)}, f32[2,128,128]{2,1,0:T(8,128)}, ...) | async-done | bytes 786448 | tf_op jit(solution)/shard_map/psum | solution.py:13
  675.4 1.7 broadcast_multiply_fusion.2
  677.1 1.9 broadcast_multiply_fusion
  (64 shorter events, 6.2 us)
Async XLA Ops:
  7.2 92.9 %all-gather.3.cloned.1.call-start = ((), (), s32[]{:S(2)}) async-start(), calls=%async_computation.3 | async-start | bytes 4456448 | tf_op jit(solution)/shard_map/all_gather | solution.py:65
  7.2 10.3 %collective-permute-start = (bf16[512,2,128]{2,1,0:T(2,128)(2,1)}, bf16[512,2,128]{2,1,0:T(2,128)(2,1)S(1)}, u32[]{:S(2)}, u32[]{:S(2)}) collective-permute-start(bf16[512,2,128]{2,1,0:T(2,128)(2,1)} %param.9), channel_id=1, source_target_pairs={{0,1},{1,2},{2,3},{3,4},{4,5},{5,6},{6,7},{7,8},{8,9},{9,10},{10,1... | collective-permute-start | bytes 786440 | tf_op jit(solution)/shard_map/ppermute | solution.py:20
  19.4 1.2 copy-start.3
  21.7 179.6 %reduce-scatter.3.cloned.1.call-start = ((), (), s32[]{:S(2)}) async-start(), calls=%async_computation.2 | async-start | bytes 8912896 | tf_op jit(solution)/shard_map/reduce_scatter | solution.py:89
  29.7 12.1 %copy-start = (bf16[512,2,128]{2,1,0:T(2,128)(2,1)S(1)}, bf16[512,2,128]{2,1,0:T(2,128)(2,1)}, u32[]{:S(2)}) copy-start(bf16[512,2,128]{2,1,0:T(2,128)(2,1)} %param.10) | copy-start | bytes 786436
  29.7 12.1 %copy-start.14 = (bf16[2,128,128]{2,1,0:T(8,128)(2,1)S(1)}, bf16[2,128,128]{2,1,0:T(8,128)(2,1)}, u32[]{:S(2)}) copy-start(bf16[2,128,128]{2,1,0:T(8,128)(2,1)} %param.16) | copy-start | bytes 196612
  66.7 0.8 copy-start.15
  66.8 217.5 %all-gather.5.cloned.1.call-start = ((), (), s32[]{:S(2)}) async-start(), calls=%async_computation.5 | async-start | bytes 4456448 | tf_op jit(solution)/shard_map/all_gather | solution.py:65
  67.8 41.9 %copy-start.1 = (bf16[512,2,128]{2,1,0:T(2,128)(2,1)S(1)}, bf16[512,2,128]{2,1,0:T(2,128)(2,1)}, u32[]{:S(2)}) copy-start(bf16[512,2,128]{2,1,0:T(2,128)(2,1)} %param.9) | copy-start | bytes 786436
  67.8 45.4 %copy-start.9 = (bf16[2,128,256]{2,1,0:T(8,128)(2,1)S(1)}, bf16[2,128,256]{2,1,0:T(8,128)(2,1)}, u32[]{:S(2)}) copy-start(bf16[2,128,256]{2,1,0:T(8,128)(2,1)} %param.14) | copy-start | bytes 393220
  67.8 57.7 %copy-start.8 = (bf16[2,128,256]{2,1,0:T(8,128)(2,1)S(1)}, bf16[2,128,256]{2,1,0:T(8,128)(2,1)}, u32[]{:S(2)}) copy-start(bf16[2,128,256]{2,1,0:T(8,128)(2,1)} %param.13) | copy-start | bytes 393220
  110.0 13.9 %collective-permute-start.1 = (bf16[512,2,128]{2,1,0:T(2,128)(2,1)S(1)}, bf16[512,2,128]{2,1,0:T(2,128)(2,1)S(1)}, u32[]{:S(2)}, u32[]{:S(2)}) collective-permute-start(bf16[512,2,128]{2,1,0:T(2,128)(2,1)S(1)} %add_convert_fusion), channel_id=1, source_target_pairs={{0,1},{1,2},{2,3},{3,4},{4,5},{5,6},{6,7},{7,8},{8,9},{9,10},{10,1... | collective-permute-start | bytes 786440 | tf_op jit(solution)/shard_map/ppermute | solution.py:20
  124.8 0.7 copy-start.5
  207.3 176.8 %reduce-scatter.5.cloned.1.call-start = ((), (), s32[]{:S(2)}) async-start(), calls=%async_computation.4 | async-start | bytes 8912896 | tf_op jit(solution)/shard_map/reduce_scatter | solution.py:89
  209.7 10.6 %collective-permute-start.2 = (f32[512,2,128]{2,0,1:T(8,128)S(1)}, f32[512,2,128]{2,0,1:T(8,128)}, u32[]{:S(2)}, u32[]{:S(2)}) collective-permute-start(f32[512,2,128]{2,0,1:T(8,128)S(1)} %fusion.33), channel_id=1, source_target_pairs={{1,0},{2,1},{3,2},{4,3},{5,4},{6,5},{7,6},{8,7},{9,8},{10,9},{11,1... | collective-permute-start | bytes 1572872 | tf_op jit(solution)/shard_map/ppermute | solution.py:20
  248.0 1.0 copy-start.7
  248.0 1.2 copy-start.11
  248.0 3.1 copy-start.6
  248.0 279.3 %all-reduce.5.cloned.1.call-start = ((), (), s32[]{:S(2)}) async-start(), calls=%async_computation.6 | async-start | bytes 1572864 | tf_op jit(solution)/shard_map/psum | solution.py:13
  254.2 132.5 %copy-start.4 = (bf16[512,2,128]{2,1,0:T(2,128)(2,1)S(1)}, bf16[512,2,128]{2,1,0:T(2,128)(2,1)}, u32[]{:S(2)}) copy-start(bf16[512,2,128]{2,1,0:T(2,128)(2,1)} %copy-done.3) | copy-start | bytes 786436
  293.6 235.4 %copy-start.2 = (f32[512,2,128]{2,0,1:T(8,128)S(1)}, f32[512,2,128]{2,0,1:T(8,128)}, u32[]{:S(2)}) copy-start(f32[512,2,128]{2,0,1:T(8,128)} %get-tuple-element.31) | copy-start | bytes 1572868
  293.6 235.4 %copy-start.10 = (bf16[2,128,256]{2,1,0:T(8,128)(2,1)S(1)}, bf16[2,128,256]{2,1,0:T(8,128)(2,1)}, u32[]{:S(2)}) copy-start(bf16[2,128,256]{2,1,0:T(8,128)(2,1)} %param.14) | copy-start | bytes 393220
  386.3 0.7 copy-start.13
  386.4 4.0 copy-start.12
  390.3 285.1 %all-reduce.7.cloned.1.call-start = ((), (), s32[]{:S(2)}) async-start(), calls=%async_computation.7 | async-start | bytes 1572864 | tf_op jit(solution)/shard_map/psum | solution.py:13
  392.7 136.3 %collective-permute-start.3 = (f32[512,2,128]{2,0,1:T(8,128)S(1)}, f32[512,2,128]{2,0,1:T(8,128)S(1)}, u32[]{:S(2)}, u32[]{:S(2)}) collective-permute-start(f32[512,2,128]{2,0,1:T(8,128)S(1)} %fusion.30), channel_id=1, source_target_pairs={{1,0},{2,1},{3,2},{4,3},{5,4},{6,5},{7,6},{8,7},{9,8},{10,9},{11,1... | collective-permute-start | bytes 1572872 | tf_op jit(solution)/shard_map/ppermute | solution.py:20
Sparse Core Ops, SparseCore 0:
  21.8 78.2 all-gather.2
  102.6 98.6 reduce-scatter.2
  207.4 76.7 all-gather.4
  286.7 97.3 reduce-scatter.4
  390.5 136.7 all-reduce.4
  530.0 145.4 all-reduce.6
